TPU v7x, 32 devices: a whole 2x2x4 slice. The times are simulated.
32 devices in a mesh: groups: 2 (over x), band: 16 (over z, y, core).
Axes of the slice: x: 2, y: 2, z: 4, core: 2. Of those that a mesh axis runs over, the one named last changes fastest.
Arguments:
- images: float32 [32, 8, 16, 32, 128], P(('groups', 'band')), parts along dimension 0, may hold values from -6 to 6
- coeffs: float32 [32, 8, 27, 3], P(('groups', 'band')), parts along dimension 0, may hold values from -3 to 3
- weights: float32 [32, 8], P(('groups', 'band')), parts along dimension 0, may hold values from 0.25 to 4
- scales: float32 [32, 8], P(('groups', 'band')), parts along dimension 0, may hold values from 0.5 to 2
- valid_epoch: int32 [32, 8], P(('groups', 'band')), parts along dimension 0, may hold values 0 or 1
- patch_owner: int32 [32, 8, 16, 1], P(('groups', 'band')), parts along dimension 0, may hold values from 0 to 15; in each aligned block of 128 rows (0 to 127, 128 to 255, ..., all dimensions but the last counted through in order) at most 16 rows name the same one
- patch_local: int32 [32, 8, 16], P(('groups', 'band')), parts along dimension 0, may hold values from 0 to 3
Outputs:
- difference: float32 [32, 8, 16, 32, 128], P(('groups', 'band')), parts along dimension 0
- templates: bfloat16 [128, 32, 128], P(('groups', 'band')), parts along dimension 0
There are 2 independent parts, one for each index of `groups`. A program takes and returns all parts, laid end to end along the dimension named above; each array names one. Nothing has to cross between parts.
Inputs may be any that keep to these rules, and one draw needn't show every extreme that they name: `patch_owner`: no band sends more than 16 of its tiles to one owner, and some band sends exactly 16 tiles to some owner; every owner receives some tile.
All inputs are finite; a program needn't handle non-finite values. No bound on the sum of `valid_epoch` on one device may be relied on, other than what follows from the above.
Results may differ from a plain program's by a relative error of at most 0.0078.
Values may be sent and summed in bfloat16 or wider, within the bound.
No kernel may reach another device: no remote copies, remote signals or barrier semaphores. Data moves between devices by JAX's collectives and lax.ppermute only.
A program may use at most 64 MiB of HBM per device.

v0:
```python
import jax
import jax.numpy as jnp
import numpy as np
from jax import lax
from jax.sharding import PartitionSpec as P

PD = 4
HALF = 9
P_SIZE = 3
sigmas = (0.75, 1.5, 3.0)
degrees = (4, 2, 2)


def kernel_matrices(tile_side):
    rows_out = lax.broadcasted_iota(jnp.int32, (tile_side, tile_side), 0)
    rows_in = lax.broadcasted_iota(jnp.int32, (tile_side, tile_side), 1)
    offset = (rows_out - rows_in).astype(jnp.float32)
    inside = (jnp.abs(rows_out - rows_in) <= HALF).astype(jnp.float32)
    taps = jnp.arange(-HALF, HALF + 1).astype(jnp.float32)
    tables = []
    for width_sigma, degree in zip(sigmas, degrees):
        normal_total = jnp.sum(jnp.exp(-taps * taps / (2.0 * width_sigma * width_sigma)))
        envelope = (
            jnp.exp(-offset * offset / (2.0 * width_sigma * width_sigma)) * inside / normal_total
        )
        for power in range(degree + 1):
            tables.append(envelope * (offset / width_sigma) ** power)
    return jnp.stack(tables)


def basis_pairs():
    kernel_list = []
    base_index = 0
    for degree in degrees:
        for column_power in range(degree + 1):
            for row_power in range(degree + 1 - column_power):
                kernel_list.append((base_index + row_power, base_index + column_power))
        base_index = base_index + degree + 1
    return kernel_list


def row_selector():
    kernel_list = basis_pairs()
    row_count = sum((degree + 1 for degree in degrees))
    table = np.zeros((len(kernel_list), row_count), np.float32)
    for basis_index, kernel_pair in enumerate(kernel_list):
        table[basis_index, kernel_pair[0]] = 1.0
    return jnp.asarray(table, jnp.float32)


def coordinates(per_epoch, tile_rows, tile_side):
    tile_index = lax.broadcasted_iota(jnp.float32, (per_epoch, tile_side), 0)
    column = lax.broadcasted_iota(jnp.float32, (per_epoch, tile_side), 1)
    across = 2.0 * (tile_index * tile_side + column + 0.5) / (per_epoch * tile_side) - 1.0
    down = 2.0 * (jnp.arange(tile_rows).astype(jnp.float32) + 0.5) / tile_rows - 1.0
    return (across, down)


def body(images, coeffs, weights, scales, valid_epoch, patch_owner, patch_local):
    band_count = lax.axis_size("band")
    epochs = images.shape[1]
    per_epoch = images.shape[2]
    tile_rows = images.shape[3]
    tile_side = images.shape[4]
    pixel_count = tile_rows * tile_side
    tile_count = epochs * per_epoch
    capacity = max(2, 2 * tile_count // band_count)
    column_kernels = kernel_matrices(tile_side)
    row_tables = kernel_matrices(tile_rows).astype(jnp.bfloat16)
    kernel_list = basis_pairs()
    column_stack = jnp.stack([column_kernels[kernel_pair[1]] for kernel_pair in kernel_list])
    selector = row_selector()
    row_count = column_kernels.shape[0]
    across, down = coordinates(per_epoch, tile_rows, tile_side)

    def one_epoch(epoch_inputs):
        tile_stack, coef_epoch = epoch_inputs
        mixing = selector[:, :, None] * coef_epoch[:, None, :]
        combined = jnp.einsum(
            "bjp,box->jxpo", mixing, column_stack, precision=lax.Precision.HIGHEST
        )
        mixer = combined.reshape(row_count * tile_side, P_SIZE * tile_side).astype(jnp.bfloat16)
        pixels = tile_stack.astype(jnp.bfloat16)
        rowed = jnp.einsum(
            "jpy,tyx->tpjx", row_tables, pixels, preferred_element_type=jnp.float32
        ).astype(jnp.bfloat16)
        flat = rowed.reshape(per_epoch, tile_rows, row_count * tile_side)
        spatial = jnp.einsum("tpk,kq->tpq", flat, mixer, preferred_element_type=jnp.float32)
        spatial = spatial.reshape(per_epoch, tile_rows, P_SIZE, tile_side)
        return (
            spatial[:, :, 0, :]
            + across[:, None, :] * spatial[:, :, 1, :]
            + down[None, :, None] * spatial[:, :, 2, :]
        )

    homogenized = lax.map(one_epoch, (images[0], coeffs[0])).reshape(tile_count, pixel_count)
    owners = patch_owner[0].reshape(tile_count)
    local_patch = patch_local[0].reshape(tile_count)
    order_index = jnp.arange(tile_count)
    earlier = (owners[:, None] == owners[None, :]) & (order_index[None, :] < order_index[:, None])
    send_rank = jnp.sum(earlier.astype(jnp.int32), axis=1)
    send_slot = owners * capacity + send_rank
    slot_total = band_count * capacity
    epoch_weight = (weights[0] * valid_epoch[0].astype(jnp.float32)).astype(jnp.bfloat16)
    tile_weight = jnp.broadcast_to(epoch_weight[:, None], (epochs, per_epoch)).reshape(tile_count)
    placement_table = (local_patch[:, None] == jnp.arange(PD)[None, :]).astype(jnp.bfloat16)
    weight_table = (
        placement_table.astype(jnp.float32) * tile_weight.astype(jnp.float32)[:, None]
    ).astype(jnp.bfloat16)
    outgoing = (
        jnp.zeros((slot_total, pixel_count), jnp.bfloat16)
        .at[send_slot]
        .set(homogenized.astype(jnp.bfloat16))
    )
    out_place = jnp.zeros((slot_total, PD), jnp.bfloat16).at[send_slot].set(placement_table)
    out_weight = jnp.zeros((slot_total, PD), jnp.bfloat16).at[send_slot].set(weight_table)
    received, got_place, got_weight = (
        lax.all_to_all(
            outgoing.reshape(band_count, capacity, pixel_count),
            "band",
            split_axis=0,
            concat_axis=0,
            tiled=True,
        ),
        lax.all_to_all(
            out_place.reshape(band_count, capacity, PD),
            "band",
            split_axis=0,
            concat_axis=0,
            tiled=True,
        ),
        lax.all_to_all(
            out_weight.reshape(band_count, capacity, PD),
            "band",
            split_axis=0,
            concat_axis=0,
            tiled=True,
        ),
    )
    flat_weight = got_weight.reshape(slot_total, PD)
    numerator = jnp.einsum(
        "sq,sk->qk",
        flat_weight,
        received.reshape(slot_total, pixel_count),
        preferred_element_type=jnp.float32,
    )
    denominator = 1.0 + jnp.sum(flat_weight.astype(jnp.float32), axis=0)
    templates = (numerator / denominator[:, None]).astype(jnp.bfloat16)
    global_patch = owners * PD + local_patch
    shard_rows = lax.all_gather(templates, "band", axis=0, tiled=True)
    row_total = shard_rows.shape[0]
    chooser = (global_patch[:, None] == jnp.arange(row_total)[None, :]).astype(jnp.bfloat16)
    matched = jnp.dot(chooser, shard_rows, preferred_element_type=jnp.float32)
    tile_scale = jnp.broadcast_to(scales[0][:, None], (epochs, per_epoch)).reshape(tile_count)
    difference = homogenized - tile_scale[:, None] * matched
    return (
        difference.reshape(1, epochs, per_epoch, tile_rows, tile_side),
        templates.reshape(PD, tile_rows, tile_side),
    )


def solution(mesh):
    return jax.shard_map(
        body,
        mesh=mesh,
        in_specs=(
            P(("groups", "band"), None, None, None, None),
            P(("groups", "band"), None, None, None),
            P(("groups", "band"), None),
            P(("groups", "band"), None),
            P(("groups", "band"), None),
            P(("groups", "band"), None, None, None),
            P(("groups", "band"), None, None),
        ),
        out_specs=(
            P(("groups", "band"), None, None, None, None),
            P(("groups", "band"), None, None),
        ),
        check_vma=False,
    )
```

profile of v0, /device:TPU:0, one launch (start us, length us, event | category | flops | bytes accessed | tf_op | source)
XLA Modules:
  0.0 226.5 jit_solution(9913890451470285794)
XLA Ops:
  2.7 1.4 fusion.47
  4.7 0.9 scatter_custom_fusion
  6.4 7.5 %all-to-all-start = ((bf16[16,16,4]{1,2,0:T(4,128)(2,1)}), bf16[16,16,4]{1,2,0:T(4,128)(2,1)}, u32[]{:S(2)}, u32[]{:S(2)}) async-start(bf16[16,16,4]{1,2,0:T(4,128)(2,1)} %copy.53), calls=%async_computation | async-start | bytes 32768 | tf_op jit(solution)/shard_map/all_to_all | solution.py:132
  15.9 1.2 constant_dynamic-update-slice_fusion.10
  18.5 1.2 constant_dynamic-update-slice_fusion.9
  19.8 1.2 constant_dynamic-update-slice_fusion.8
  21.0 1.2 constant_dynamic-update-slice_fusion.7
  22.3 1.3 constant_dynamic-update-slice_fusion.6
  23.5 1.2 constant_dynamic-update-slice_fusion.5
  24.7 1.2 constant_dynamic-update-slice_fusion.4
  26.0 1.2 constant_dynamic-update-slice_fusion.3
  27.2 1.2 constant_dynamic-update-slice_fusion.2
  28.5 1.2 constant_dynamic-update-slice_fusion.1
  29.7 1.2 constant_dynamic-update-slice_fusion
  31.0 2.8 %bitcast_convert_fusion.3 = bf16[8,16,32,128]{3,2,1,0:T(8,128)(2,1)} fusion(f32[1,8,16,32,128]{4,3,2,1,0:T(8,128)} %param.10), kind=kLoop, calls=%fused_computation.143 | loop fusion | flops 524288 | bytes 3145728
  51.4 2.3 %copy.50 = f32[27,128,128]{2,0,1:T(8,128)} copy(f32[27,128,128]{2,1,0:T(8,128)S(1)} %constant_dynamic-update-slice_fusion.11) | data formatting | bytes 3538944
  53.8 85.4 %while.12 = (s32[]{:T(128)}, f32[8,16,32,128]{3,2,1,0:T(8,128)}, bf16[8,16,32,128]{3,2,1,0:T(8,128)(2,1)}, bf16[11,32,32]{2,1,0:T(8,128)(2,1)}, f32[8,27,3]{1,2,...) while((s32[]{:T(128)}, f32[8,16,32,128]{3,2,1,0:T(8,128)}, ...), condition=%wide.region_4.0_spmd.clone.clone, body=%wide.region_3.0_spmd.sunk.clone.clone.sunk | while | flops 776496128 | bytes 16842668 | solution.py:96
  54.9 1.5 fusion.69
  57.1 1.0 reshape.451
  58.1 4.2 %fusion.68 = bf16[11,3,128,128]{3,0,2,1:T(8,128)(2,1)S(1)} fusion(f32[27,128,128]{2,0,1:T(8,128)} %get-tuple-element.184, f32[27,3]{0,1:T(4,128)} %dynamic-slice_bitcast_fusion.2, f32[27,11]{0,1:T(8,128)S(1)} %get-tuple-element.187), kind=kOutput, calls=%fused_computation.6.clone.1 | convolution fusion | flops 175719296 | bytes 2852328 | tf_op jit(solution)/shard_map/while/body/eval_jaxpr/bjp,box->jxpo/dot_general | solution.py:79
  62.7 0.9 fusion.70
  63.6 0.8 fusion.71
  65.6 1.5 fusion.69
  67.8 1.0 reshape.451
  68.8 4.2 %fusion.68 = bf16[11,3,128,128]{3,0,2,1:T(8,128)(2,1)S(1)} fusion(f32[27,128,128]{2,0,1:T(8,128)} %get-tuple-element.184, f32[27,3]{0,1:T(4,128)} %dynamic-slice_bitcast_fusion.2, f32[27,11]{0,1:T(8,128)S(1)} %get-tuple-element.187), kind=kOutput, calls=%fused_computation.6.clone.1 | convolution fusion | flops 175719296 | bytes 2852328 | tf_op jit(solution)/shard_map/while/body/eval_jaxpr/bjp,box->jxpo/dot_general | solution.py:79
  73.3 0.9 fusion.70
  74.3 0.8 fusion.71
  76.3 1.5 fusion.69
  78.5 1.0 reshape.451
  79.4 4.2 %fusion.68 = bf16[11,3,128,128]{3,0,2,1:T(8,128)(2,1)S(1)} fusion(f32[27,128,128]{2,0,1:T(8,128)} %get-tuple-element.184, f32[27,3]{0,1:T(4,128)} %dynamic-slice_bitcast_fusion.2, f32[27,11]{0,1:T(8,128)S(1)} %get-tuple-element.187), kind=kOutput, calls=%fused_computation.6.clone.1 | convolution fusion | flops 175719296 | bytes 2852328 | tf_op jit(solution)/shard_map/while/body/eval_jaxpr/bjp,box->jxpo/dot_general | solution.py:79
  84.0 0.9 fusion.70
  85.0 0.8 fusion.71
  87.0 1.5 fusion.69
  89.2 1.0 reshape.451
  90.1 4.2 %fusion.68 = bf16[11,3,128,128]{3,0,2,1:T(8,128)(2,1)S(1)} fusion(f32[27,128,128]{2,0,1:T(8,128)} %get-tuple-element.184, f32[27,3]{0,1:T(4,128)} %dynamic-slice_bitcast_fusion.2, f32[27,11]{0,1:T(8,128)S(1)} %get-tuple-element.187), kind=kOutput, calls=%fused_computation.6.clone.1 | convolution fusion | flops 175719296 | bytes 2852328 | tf_op jit(solution)/shard_map/while/body/eval_jaxpr/bjp,box->jxpo/dot_general | solution.py:79
  94.7 0.9 fusion.70
  95.7 0.8 fusion.71
  97.6 1.5 fusion.69
  99.8 1.0 reshape.451
  100.8 4.2 %fusion.68 = bf16[11,3,128,128]{3,0,2,1:T(8,128)(2,1)S(1)} fusion(f32[27,128,128]{2,0,1:T(8,128)} %get-tuple-element.184, f32[27,3]{0,1:T(4,128)} %dynamic-slice_bitcast_fusion.2, f32[27,11]{0,1:T(8,128)S(1)} %get-tuple-element.187), kind=kOutput, calls=%fused_computation.6.clone.1 | convolution fusion | flops 175719296 | bytes 2852328 | tf_op jit(solution)/shard_map/while/body/eval_jaxpr/bjp,box->jxpo/dot_general | solution.py:79
  105.4 0.9 fusion.70
  106.3 0.8 fusion.71
  108.3 1.5 fusion.69
  110.5 1.0 reshape.451
  111.5 4.2 %fusion.68 = bf16[11,3,128,128]{3,0,2,1:T(8,128)(2,1)S(1)} fusion(f32[27,128,128]{2,0,1:T(8,128)} %get-tuple-element.184, f32[27,3]{0,1:T(4,128)} %dynamic-slice_bitcast_fusion.2, f32[27,11]{0,1:T(8,128)S(1)} %get-tuple-element.187), kind=kOutput, calls=%fused_computation.6.clone.1 | convolution fusion | flops 175719296 | bytes 2852328 | tf_op jit(solution)/shard_map/while/body/eval_jaxpr/bjp,box->jxpo/dot_general | solution.py:79
  116.0 0.9 fusion.70
  117.0 0.8 fusion.71
  119.0 1.5 fusion.69
  121.2 1.0 reshape.451
  122.2 4.2 %fusion.68 = bf16[11,3,128,128]{3,0,2,1:T(8,128)(2,1)S(1)} fusion(f32[27,128,128]{2,0,1:T(8,128)} %get-tuple-element.184, f32[27,3]{0,1:T(4,128)} %dynamic-slice_bitcast_fusion.2, f32[27,11]{0,1:T(8,128)S(1)} %get-tuple-element.187), kind=kOutput, calls=%fused_computation.6.clone.1 | convolution fusion | flops 175719296 | bytes 2852328 | tf_op jit(solution)/shard_map/while/body/eval_jaxpr/bjp,box->jxpo/dot_general | solution.py:79
  126.7 0.9 fusion.70
  127.7 0.8 fusion.71
  129.7 1.5 fusion.69
  131.9 1.0 reshape.451
  132.8 4.2 %fusion.68 = bf16[11,3,128,128]{3,0,2,1:T(8,128)(2,1)S(1)} fusion(f32[27,128,128]{2,0,1:T(8,128)} %get-tuple-element.184, f32[27,3]{0,1:T(4,128)} %dynamic-slice_bitcast_fusion.2, f32[27,11]{0,1:T(8,128)S(1)} %get-tuple-element.187), kind=kOutput, calls=%fused_computation.6.clone.1 | convolution fusion | flops 175719296 | bytes 2852328 | tf_op jit(solution)/shard_map/while/body/eval_jaxpr/bjp,box->jxpo/dot_general | solution.py:79
  137.4 0.9 fusion.70
  139.2 5.7 %scatter_custom_fusion.1 = bf16[256,4096]{1,0:T(8,128)(2,1)} fusion(s32[128]{0:T(128)} %copy-done.12, f32[16,8,32,128]{3,2,1,0:T(8,128)} %bitcast.141, bf16[]{:T(256)} %constant.93.clone.1), kind=kCustom, calls=%fused_computation.38 | custom fusion | bytes 4194816 | tf_op jit(solution)/shard_map/scatter | solution.py:113
  144.9 6.2 %all-to-all-start.1 = ((bf16[16,16,4096]{2,1,0:T(8,128)(2,1)}), bf16[16,16,4096]{2,1,0:T(8,128)(2,1)}, u32[]{:S(2)}, u32[]{:S(2)}) async-start(bf16[16,16,4096]{2,1,0:T(8,128)(2,1)} %bitcast.7), calls=%async_computation.1 | async-start | bytes 4194304 | tf_op jit(solution)/shard_map/all_to_all | solution.py:118
  151.3 0.8 convert_reduce_fusion.1
  152.1 40.0 %all-to-all-done.1 = bf16[16,16,4096]{2,1,0:T(8,128)(2,1)} async-done(((bf16[16,16,4096]{2,1,0:T(8,128)(2,1)}), bf16[16,16,4096]{2,1,0:T(8,128)(2,1)}, u32[]{:S(2)}, u32[]{:S(2)}) %all-to-all-start.1) | async-done | bytes 2097184 | tf_op jit(solution)/shard_map/all_to_all | solution.py:118
  192.1 2.0 fusion.27
  194.8 28.4 %all-gather = bf16[16,4,4096]{2,1,0:T(4,128)(2,1)S(1)} all-gather(bf16[1,4,4096]{2,1,0:T(4,128)(2,1)S(1)} %bitcast.145), channel_id=1, replica_groups=mesh['groups'=2,'band'=16] {'band'}, dimensions={0}, use_global_device_ids=true | all-gather | bytes 557056 | tf_op jit(solution)/shard_map/all_gather | solution.py:150
  223.4 1.5 fusion.28
  224.8 1.7 copy.65
  (189 shorter events, 43.7 us)
Async XLA Ops:
  1.4 3.2 %copy-start.7 = (s32[128]{0:T(128)}, s32[128]{0:T(128)S(1)}, u32[]{:S(2)}) copy-start(s32[128]{0:T(128)S(1)} %reshape_squeeze.7) | copy-start | bytes 1540
  4.2 0.5 copy-start.10
  4.7 11.1 %copy-start.12 = (s32[128]{0:T(128)}, s32[128]{0:T(128)S(1)}, u32[]{:S(2)}) copy-start(s32[128]{0:T(128)S(1)} %fusion.46) | copy-start | bytes 1540
  6.4 138.5 %all-to-all-start = ((bf16[16,16,4]{1,2,0:T(4,128)(2,1)}), bf16[16,16,4]{1,2,0:T(4,128)(2,1)}, u32[]{:S(2)}, u32[]{:S(2)}) async-start(bf16[16,16,4]{1,2,0:T(4,128)(2,1)} %copy.53), calls=%async_computation | async-start | bytes 32768 | tf_op jit(solution)/shard_map/all_to_all | solution.py:132
  51.4 2.4 %copy-start.1 = (f32[27,11]{0,1:T(8,128)S(1)}, f32[27,11]{0,1:T(8,128)}, u32[]{:S(2)}) copy-start(f32[27,11]{0,1:T(8,128)} %constant.97.clone..sunk.3) | copy-start | bytes 3568
  53.8 1.2 copy-start.2
  53.8 1.2 copy-start.5
  62.6 1.0 copy-start.4
  62.6 1.8 copy-start.3
  62.6 1.8 copy-start.6
  64.4 1.2 copy-start.2
  64.4 1.2 copy-start.5
  73.3 1.0 copy-start.4
  73.3 1.8 copy-start.3
  73.3 1.8 copy-start.6
  75.1 1.2 copy-start.2
  75.1 1.2 copy-start.5
  84.0 1.0 copy-start.4
  84.0 1.8 copy-start.3
  84.0 1.8 copy-start.6
  85.8 1.2 copy-start.2
  85.8 1.2 copy-start.5
  94.7 1.0 copy-start.4
  94.7 1.8 copy-start.3
  94.7 1.8 copy-start.6
  96.5 1.2 copy-start.2
  96.5 1.2 copy-start.5
  105.3 1.0 copy-start.4
  105.3 1.8 copy-start.3
  105.4 1.8 copy-start.6
  107.1 1.2 copy-start.2
  107.1 1.2 copy-start.5
  116.0 1.0 copy-start.4
  116.0 1.8 copy-start.3
  116.0 1.8 copy-start.6
  117.8 1.2 copy-start.2
  117.8 1.2 copy-start.5
  126.7 1.0 copy-start.4
  126.7 1.8 copy-start.3
  126.7 1.8 copy-start.6
  128.5 1.2 copy-start.2
  128.5 1.2 copy-start.5
  137.4 1.0 copy-start.4
  137.4 1.8 copy-start.3
  137.4 1.8 copy-start.6
  144.9 6.2 %copy-start.9 = (f32[1,8]{1,0:T(1,128)S(1)}, f32[1,8]{1,0:T(1,128)}, u32[]{:S(2)}) copy-start(f32[1,8]{1,0:T(1,128)} %param.13) | copy-start | bytes 100
  144.9 6.3 %copy-start.8 = (s32[128]{0:T(128)S(1)}, s32[128]{0:T(128)}, u32[]{:S(2)}) copy-start(s32[128]{0:T(128)} %copy-done.7) | copy-start | bytes 1540
  144.9 6.3 %copy-start.11 = (s32[128]{0:T(128)S(1)}, s32[128]{0:T(128)}, u32[]{:S(2)}) copy-start(s32[128]{0:T(128)} %copy-done.10) | copy-start | bytes 1540
  144.9 47.2 %all-to-all-start.1 = ((bf16[16,16,4096]{2,1,0:T(8,128)(2,1)}), bf16[16,16,4096]{2,1,0:T(8,128)(2,1)}, u32[]{:S(2)}, u32[]{:S(2)}) async-start(bf16[16,16,4096]{2,1,0:T(8,128)(2,1)} %bitcast.7), calls=%async_computation.1 | async-start | bytes 4194304 | tf_op jit(solution)/shard_map/all_to_all | solution.py:118
  152.1 71.2 %copy-start = (f32[8,16,32,128]{3,2,1,0:T(8,128)S(1)}, f32[8,16,32,128]{3,2,1,0:T(8,128)}, u32[]{:S(2)}) copy-start(f32[8,16,32,128]{3,2,1,0:T(8,128)} %get-tuple-element.49) | copy-start | bytes 6291460
where the time goes:
time: 228 us; the launch traced here: 227 us
  matrix products  56.5 us (25%)
  other arithmetic  51.1 us (22%)
  waiting for transfers between devices  40 us (18%)
  local copies, waits for them, and re-layouts  35.3 us (15%)
  blocking collectives  28.4 us (12%)
  starting transfers between devices  13.6 us (6%)
    all_to_all x1, waiting for transfers between devices, body(): lax.all_to_all(outgoing.reshape(band_count, capacity, pixel_count), 'band...  40 us
    unnamed x38, other arithmetic  34 us
    dot_general x8, matrix products, one_epoch(): jnp.einsum('bjp,box->jxpo', mixing, column_stack, precision=lax.Precision...  33.7 us
    all_gather x1, blocking collectives, body(): shard_rows = lax.all_gather(templates, 'band', axis=0, tiled=True)  28.4 us
    dot_general x8, matrix products, one_epoch(): jnp.einsum('jpy,tyx->tpjx', row_tables, pixels, preferred_element_type=jn...  11.7 us
    reshape x8, local copies, waits for them, and re-layouts, one_epoch(): flat = rowed.reshape(per_epoch, tile_rows, row_count * tile_side)  7.69 us
    dot_general x8, matrix products, one_epoch(): jnp.einsum('tpk,kq->tpq', flat, mixer, preferred_element_type=jnp.float32)  7.57 us
    all_to_all x1, starting transfers between devices, body(): lax.all_to_all(out_weight.reshape(band_count, capacity, PD), 'band', spli...  7.46 us
  transfers between devices with their start and end apart: 2, of which 1 were waited for; matrix products, arithmetic and copies ran while one was open for 58% of the time, Pallas kernels for 0%

commit v1 on v0

--- a/solution.py
+++ b/solution.py
@@ -147,7 +147,14 @@
     denominator = 1.0 + jnp.sum(flat_weight.astype(jnp.float32), axis=0)
     templates = (numerator / denominator[:, None]).astype(jnp.bfloat16)
     global_patch = owners * PD + local_patch
-    shard_rows = lax.all_gather(templates, "band", axis=0, tiled=True)
+    size = lax.axis_size("band")
+    hops = [(i, (i + 1) % size) for i in range(size)]
+    pieces = [templates]
+    for stride in range(1, size):
+        pieces = [lax.ppermute(pieces[0], "band", hops), *pieces]
+    full = jnp.concatenate(pieces, axis=0)
+    shift = (lax.axis_index("band") + 1) * pieces[-1].shape[0]
+    shard_rows = jnp.roll(full, shift, axis=0)
     row_total = shard_rows.shape[0]
     chooser = (global_patch[:, None] == jnp.arange(row_total)[None, :]).astype(jnp.bfloat16)
     matched = jnp.dot(chooser, shard_rows, preferred_element_type=jnp.float32)

time: 228 us -> 300 us (1.32)
  waiting for transfers between devices: 40 us -> 134 us
  blocking collectives: 28.4 us -> 0 us
  local copies, waits for them, and re-layouts: 35.3 us -> 39.7 us
    ppermute x0 -> x15, waiting for transfers between devices: none -> 94.2 us  [body(): pieces = [lax.ppermute(pieces[0], 'band', hops), *pieces]]
    all_gather x1 -> x0, blocking collectives: 28.4 us -> none  [body(): shard_rows = lax.all_gather(templates, 'band', axis=0, tiled=True)]
    concatenate x0 -> x1, local copies, waits for them, and re-layouts: none -> 4.1 us  [body(): shard_rows = jnp.roll(full, shift, axis=0)]
    unnamed x22 -> x27, local copies, waits for them, and re-layouts: 6.17 us -> 6.02 us
  transfers between devices with their start and end apart: 2 -> 17, of which waited for: 1 -> 16; matrix products, arithmetic and copies ran while one was open for 58% -> 44% of each run, Pallas kernels for 0% -> 0%
where the time goes in v1:
time: 300 us; the launch traced here: 299 us
  waiting for transfers between devices  134 us (45%)
  matrix products  56.5 us (19%)
  other arithmetic  51.9 us (17%)
  local copies, waits for them, and re-layouts  39.7 us (13%)
  starting transfers between devices  14.5 us (5%)
    ppermute x15, waiting for transfers between devices, body(): pieces = [lax.ppermute(pieces[0], 'band', hops), *pieces]  94.2 us
    all_to_all x1, waiting for transfers between devices, body(): lax.all_to_all(outgoing.reshape(band_count, capacity, pixel_count), 'band...  40.1 us
    unnamed x38, other arithmetic  34.3 us
    dot_general x8, matrix products, one_epoch(): jnp.einsum('bjp,box->jxpo', mixing, column_stack, precision=lax.Precision...  33.7 us
    dot_general x8, matrix products, one_epoch(): jnp.einsum('jpy,tyx->tpjx', row_tables, pixels, preferred_element_type=jn...  11.7 us
    reshape x8, local copies, waits for them, and re-layouts, one_epoch(): flat = rowed.reshape(per_epoch, tile_rows, row_count * tile_side)  7.69 us
    dot_general x8, matrix products, one_epoch(): jnp.einsum('tpk,kq->tpq', flat, mixer, preferred_element_type=jnp.float32)  7.58 us
    all_to_all x1, starting transfers between devices, body(): lax.all_to_all(out_weight.reshape(band_count, capacity, PD), 'band', spli...  7.46 us
  transfers between devices with their start and end apart: 17, of which 16 were waited for; matrix products, arithmetic and copies ran while one was open for 44% of the time, Pallas kernels for 0%

profile of v1, /device:TPU:0, one launch (start us, length us, event | category | flops | bytes accessed | tf_op | source)
XLA Modules:
  0.0 298.6 jit_solution(16633729965661996397)
XLA Ops:
  2.7 1.4 fusion.49
  6.4 7.5 %all-to-all-start = ((bf16[16,16,4]{1,2,0:T(4,128)(2,1)}), bf16[16,16,4]{1,2,0:T(4,128)(2,1)}, u32[]{:S(2)}, u32[]{:S(2)}) async-start(bf16[16,16,4]{1,2,0:T(4,128)(2,1)} %copy.45), calls=%async_computation | async-start | bytes 32768 | tf_op jit(solution)/shard_map/all_to_all | solution.py:132
  15.9 1.2 constant_dynamic-update-slice_fusion.10
  18.5 1.2 constant_dynamic-update-slice_fusion.9
  19.8 1.2 constant_dynamic-update-slice_fusion.8
  21.0 1.2 constant_dynamic-update-slice_fusion.7
  22.2 1.2 constant_dynamic-update-slice_fusion.6
  23.5 1.2 constant_dynamic-update-slice_fusion.5
  24.7 1.2 constant_dynamic-update-slice_fusion.4
  25.9 1.2 constant_dynamic-update-slice_fusion.3
  27.2 1.3 constant_dynamic-update-slice_fusion.2
  28.5 1.3 constant_dynamic-update-slice_fusion.1
  29.8 1.3 constant_dynamic-update-slice_fusion
  31.1 2.8 bitcast_convert_fusion.3
  51.8 2.3 copy.42
  54.1 86.3 %while.12 = (s32[]{:T(128)}, f32[8,16,32,128]{3,2,1,0:T(8,128)}, bf16[8,16,32,128]{3,2,1,0:T(8,128)(2,1)}, bf16[11,32,32]{2,1,0:T(8,128)(2,1)}, f32[8,27,3]{1,2,...) while((s32[]{:T(128)}, f32[8,16,32,128]{3,2,1,0:T(8,128)}, ...), condition=%wide.region_4.0_spmd.clone.clone, body=%wide.region_3.0_spmd.sunk.clone.clone.sunk | while | flops 776496128 | bytes 16842668 | solution.py:96
  55.4 1.5 fusion.70
  57.6 1.0 reshape.449
  58.5 4.2 %fusion.69 = bf16[11,3,128,128]{3,0,2,1:T(8,128)(2,1)S(1)} fusion(f32[27,128,128]{2,0,1:T(8,128)} %get-tuple-element.184, f32[27,3]{0,1:T(4,128)} %dynamic-slice_bitcast_fusion.2, f32[27,11]{0,1:T(8,128)S(1)} %get-tuple-element.187), kind=kOutput, calls=%fused_computation.6.clone.1 | convolution fusion | flops 175719296 | bytes 2852328 | tf_op jit(solution)/shard_map/while/body/eval_jaxpr/bjp,box->jxpo/dot_general | solution.py:79
  66.2 1.5 fusion.70
  68.4 1.0 reshape.449
  69.3 4.2 %fusion.69 = bf16[11,3,128,128]{3,0,2,1:T(8,128)(2,1)S(1)} fusion(f32[27,128,128]{2,0,1:T(8,128)} %get-tuple-element.184, f32[27,3]{0,1:T(4,128)} %dynamic-slice_bitcast_fusion.2, f32[27,11]{0,1:T(8,128)S(1)} %get-tuple-element.187), kind=kOutput, calls=%fused_computation.6.clone.1 | convolution fusion | flops 175719296 | bytes 2852328 | tf_op jit(solution)/shard_map/while/body/eval_jaxpr/bjp,box->jxpo/dot_general | solution.py:79
  73.9 1.0 fusion.71
  77.0 1.5 fusion.70
  79.2 1.0 reshape.449
  80.1 4.2 %fusion.69 = bf16[11,3,128,128]{3,0,2,1:T(8,128)(2,1)S(1)} fusion(f32[27,128,128]{2,0,1:T(8,128)} %get-tuple-element.184, f32[27,3]{0,1:T(4,128)} %dynamic-slice_bitcast_fusion.2, f32[27,11]{0,1:T(8,128)S(1)} %get-tuple-element.187), kind=kOutput, calls=%fused_computation.6.clone.1 | convolution fusion | flops 175719296 | bytes 2852328 | tf_op jit(solution)/shard_map/while/body/eval_jaxpr/bjp,box->jxpo/dot_general | solution.py:79
  87.7 1.5 fusion.70
  89.9 1.0 reshape.449
  90.9 4.2 %fusion.69 = bf16[11,3,128,128]{3,0,2,1:T(8,128)(2,1)S(1)} fusion(f32[27,128,128]{2,0,1:T(8,128)} %get-tuple-element.184, f32[27,3]{0,1:T(4,128)} %dynamic-slice_bitcast_fusion.2, f32[27,11]{0,1:T(8,128)S(1)} %get-tuple-element.187), kind=kOutput, calls=%fused_computation.6.clone.1 | convolution fusion | flops 175719296 | bytes 2852328 | tf_op jit(solution)/shard_map/while/body/eval_jaxpr/bjp,box->jxpo/dot_general | solution.py:79
  98.5 1.5 fusion.70
  100.7 1.0 reshape.449
  101.7 4.2 %fusion.69 = bf16[11,3,128,128]{3,0,2,1:T(8,128)(2,1)S(1)} fusion(f32[27,128,128]{2,0,1:T(8,128)} %get-tuple-element.184, f32[27,3]{0,1:T(4,128)} %dynamic-slice_bitcast_fusion.2, f32[27,11]{0,1:T(8,128)S(1)} %get-tuple-element.187), kind=kOutput, calls=%fused_computation.6.clone.1 | convolution fusion | flops 175719296 | bytes 2852328 | tf_op jit(solution)/shard_map/while/body/eval_jaxpr/bjp,box->jxpo/dot_general | solution.py:79
  109.3 1.5 fusion.70
  111.5 1.0 reshape.449
  112.5 4.2 %fusion.69 = bf16[11,3,128,128]{3,0,2,1:T(8,128)(2,1)S(1)} fusion(f32[27,128,128]{2,0,1:T(8,128)} %get-tuple-element.184, f32[27,3]{0,1:T(4,128)} %dynamic-slice_bitcast_fusion.2, f32[27,11]{0,1:T(8,128)S(1)} %get-tuple-element.187), kind=kOutput, calls=%fused_computation.6.clone.1 | convolution fusion | flops 175719296 | bytes 2852328 | tf_op jit(solution)/shard_map/while/body/eval_jaxpr/bjp,box->jxpo/dot_general | solution.py:79
  120.1 1.5 fusion.70
  122.3 1.0 reshape.449
  123.3 4.2 %fusion.69 = bf16[11,3,128,128]{3,0,2,1:T(8,128)(2,1)S(1)} fusion(f32[27,128,128]{2,0,1:T(8,128)} %get-tuple-element.184, f32[27,3]{0,1:T(4,128)} %dynamic-slice_bitcast_fusion.2, f32[27,11]{0,1:T(8,128)S(1)} %get-tuple-element.187), kind=kOutput, calls=%fused_computation.6.clone.1 | convolution fusion | flops 175719296 | bytes 2852328 | tf_op jit(solution)/shard_map/while/body/eval_jaxpr/bjp,box->jxpo/dot_general | solution.py:79
  130.9 1.5 fusion.70
  133.1 1.0 reshape.449
  134.1 4.2 %fusion.69 = bf16[11,3,128,128]{3,0,2,1:T(8,128)(2,1)S(1)} fusion(f32[27,128,128]{2,0,1:T(8,128)} %get-tuple-element.184, f32[27,3]{0,1:T(4,128)} %dynamic-slice_bitcast_fusion.2, f32[27,11]{0,1:T(8,128)S(1)} %get-tuple-element.187), kind=kOutput, calls=%fused_computation.6.clone.1 | convolution fusion | flops 175719296 | bytes 2852328 | tf_op jit(solution)/shard_map/while/body/eval_jaxpr/bjp,box->jxpo/dot_general | solution.py:79
  140.4 5.8 %scatter_custom_fusion.1 = bf16[256,4096]{1,0:T(8,128)(2,1)} fusion(s32[128]{0:T(128)} %copy-done.15, f32[16,8,32,128]{3,2,1,0:T(8,128)} %bitcast.139, bf16[]{:T(256)} %constant.116.clone.1), kind=kCustom, calls=%fused_computation.38 | custom fusion | bytes 4194816 | tf_op jit(solution)/shard_map/scatter | solution.py:113
  146.2 6.0 %all-to-all-start.1 = ((bf16[16,16,4096]{2,1,0:T(8,128)(2,1)}), bf16[16,16,4096]{2,1,0:T(8,128)(2,1)}, u32[]{:S(2)}, u32[]{:S(2)}) async-start(bf16[16,16,4096]{2,1,0:T(8,128)(2,1)} %bitcast.7), calls=%async_computation.1 | async-start | bytes 4194304 | tf_op jit(solution)/shard_map/all_to_all | solution.py:118
  153.1 40.1 %all-to-all-done.1 = bf16[16,16,4096]{2,1,0:T(8,128)(2,1)} async-done(((bf16[16,16,4096]{2,1,0:T(8,128)(2,1)}), bf16[16,16,4096]{2,1,0:T(8,128)(2,1)}, u32[]{:S(2)}, u32[]{:S(2)}) %all-to-all-start.1) | async-done | bytes 2097184 | tf_op jit(solution)/shard_map/all_to_all | solution.py:118
  193.2 2.0 fusion.27
  195.3 1.0 collective-permute-start
  196.2 10.5 %collective-permute-done = bf16[4,4096]{1,0:T(4,128)(2,1)S(1)} collective-permute-done((bf16[4,4096]{1,0:T(4,128)(2,1)S(1)}, bf16[4,4096]{1,0:T(4,128)(2,1)S(1)}, u32[]{:S(2)}, u32[]{:S(2)}) %collective-permute-start) | collective-permute-done | bytes 32800 | tf_op jit(solution)/shard_map/ppermute | solution.py:154
  206.7 6.0 %collective-permute-done.1 = bf16[4,4096]{1,0:T(4,128)(2,1)S(1)} collective-permute-done((bf16[4,4096]{1,0:T(4,128)(2,1)S(1)}, bf16[4,4096]{1,0:T(4,128)(2,1)S(1)}, u32[]{:S(2)}, u32[]{:S(2)}) %collective-permute-start.1) | collective-permute-done | bytes 32800 | tf_op jit(solution)/shard_map/ppermute | solution.py:154
  212.7 6.0 %collective-permute-done.2 = bf16[4,4096]{1,0:T(4,128)(2,1)S(1)} collective-permute-done((bf16[4,4096]{1,0:T(4,128)(2,1)S(1)}, bf16[4,4096]{1,0:T(4,128)(2,1)S(1)}, u32[]{:S(2)}, u32[]{:S(2)}) %collective-permute-start.2) | collective-permute-done | bytes 32800 | tf_op jit(solution)/shard_map/ppermute | solution.py:154
  218.8 6.0 %collective-permute-done.3 = bf16[4,4096]{1,0:T(4,128)(2,1)S(1)} collective-permute-done((bf16[4,4096]{1,0:T(4,128)(2,1)S(1)}, bf16[4,4096]{1,0:T(4,128)(2,1)S(1)}, u32[]{:S(2)}, u32[]{:S(2)}) %collective-permute-start.3) | collective-permute-done | bytes 32800 | tf_op jit(solution)/shard_map/ppermute | solution.py:154
  224.8 6.0 %collective-permute-done.4 = bf16[4,4096]{1,0:T(4,128)(2,1)S(1)} collective-permute-done((bf16[4,4096]{1,0:T(4,128)(2,1)S(1)}, bf16[4,4096]{1,0:T(4,128)(2,1)S(1)}, u32[]{:S(2)}, u32[]{:S(2)}) %collective-permute-start.4) | collective-permute-done | bytes 32800 | tf_op jit(solution)/shard_map/ppermute | solution.py:154
  230.9 6.0 %collective-permute-done.5 = bf16[4,4096]{1,0:T(4,128)(2,1)S(1)} collective-permute-done((bf16[4,4096]{1,0:T(4,128)(2,1)S(1)}, bf16[4,4096]{1,0:T(4,128)(2,1)S(1)}, u32[]{:S(2)}, u32[]{:S(2)}) %collective-permute-start.5) | collective-permute-done | bytes 32800 | tf_op jit(solution)/shard_map/ppermute | solution.py:154
  236.9 6.0 %collective-permute-done.6 = bf16[4,4096]{1,0:T(4,128)(2,1)S(1)} collective-permute-done((bf16[4,4096]{1,0:T(4,128)(2,1)S(1)}, bf16[4,4096]{1,0:T(4,128)(2,1)S(1)}, u32[]{:S(2)}, u32[]{:S(2)}) %collective-permute-start.6) | collective-permute-done | bytes 32800 | tf_op jit(solution)/shard_map/ppermute | solution.py:154
  242.9 6.0 %collective-permute-done.7 = bf16[4,4096]{1,0:T(4,128)(2,1)S(1)} collective-permute-done((bf16[4,4096]{1,0:T(4,128)(2,1)S(1)}, bf16[4,4096]{1,0:T(4,128)(2,1)S(1)}, u32[]{:S(2)}, u32[]{:S(2)}) %collective-permute-start.7) | collective-permute-done | bytes 32800 | tf_op jit(solution)/shard_map/ppermute | solution.py:154
  249.0 6.0 %collective-permute-done.8 = bf16[4,4096]{1,0:T(4,128)(2,1)S(1)} collective-permute-done((bf16[4,4096]{1,0:T(4,128)(2,1)S(1)}, bf16[4,4096]{1,0:T(4,128)(2,1)S(1)}, u32[]{:S(2)}, u32[]{:S(2)}) %collective-permute-start.8) | collective-permute-done | bytes 32800 | tf_op jit(solution)/shard_map/ppermute | solution.py:154
  255.0 6.0 %collective-permute-done.9 = bf16[4,4096]{1,0:T(4,128)(2,1)S(1)} collective-permute-done((bf16[4,4096]{1,0:T(4,128)(2,1)S(1)}, bf16[4,4096]{1,0:T(4,128)(2,1)S(1)}, u32[]{:S(2)}, u32[]{:S(2)}) %collective-permute-start.9) | collective-permute-done | bytes 32800 | tf_op jit(solution)/shard_map/ppermute | solution.py:154
  261.0 6.0 %collective-permute-done.10 = bf16[4,4096]{1,0:T(4,128)(2,1)S(1)} collective-permute-done((bf16[4,4096]{1,0:T(4,128)(2,1)S(1)}, bf16[4,4096]{1,0:T(4,128)(2,1)S(1)}, u32[]{:S(2)}, u32[]{:S(2)}) %collective-permute-start.10) | collective-permute-done | bytes 32800 | tf_op jit(solution)/shard_map/ppermute | solution.py:154
  267.1 6.0 %collective-permute-done.11 = bf16[4,4096]{1,0:T(4,128)(2,1)S(1)} collective-permute-done((bf16[4,4096]{1,0:T(4,128)(2,1)S(1)}, bf16[4,4096]{1,0:T(4,128)(2,1)S(1)}, u32[]{:S(2)}, u32[]{:S(2)}) %collective-permute-start.11) | collective-permute-done | bytes 32800 | tf_op jit(solution)/shard_map/ppermute | solution.py:154
  273.1 6.0 %collective-permute-done.12 = bf16[4,4096]{1,0:T(4,128)(2,1)S(1)} collective-permute-done((bf16[4,4096]{1,0:T(4,128)(2,1)S(1)}, bf16[4,4096]{1,0:T(4,128)(2,1)S(1)}, u32[]{:S(2)}, u32[]{:S(2)}) %collective-permute-start.12) | collective-permute-done | bytes 32800 | tf_op jit(solution)/shard_map/ppermute | solution.py:154
  279.2 6.0 %collective-permute-done.13 = bf16[4,4096]{1,0:T(4,128)(2,1)S(1)} collective-permute-done((bf16[4,4096]{1,0:T(4,128)(2,1)S(1)}, bf16[4,4096]{1,0:T(4,128)(2,1)S(1)}, u32[]{:S(2)}, u32[]{:S(2)}) %collective-permute-start.13) | collective-permute-done | bytes 32800 | tf_op jit(solution)/shard_map/ppermute | solution.py:154
  286.0 5.3 %collective-permute-done.14 = bf16[4,4096]{1,0:T(4,128)(2,1)} collective-permute-done((bf16[4,4096]{1,0:T(4,128)(2,1)S(1)}, bf16[4,4096]{1,0:T(4,128)(2,1)}, u32[]{:S(2)}, u32[]{:S(2)}) %collective-permute-start.14) | collective-permute-done | bytes 32800 | tf_op jit(solution)/shard_map/ppermute | solution.py:154
  291.3 4.1 %concatenate.6 = bf16[128,4096]{1,0:T(8,128)(2,1)S(1)} concatenate(bf16[4,4096]{1,0:T(4,128)(2,1)} %collective-permute-done.14, bf16[4,4096]{1,0:T(4,128)(2,1)} %copy-done.4, bf16[4,4096]{1,0:T(4,128)(2,1)} %copy-done.3, bf16[4,4096]{1,0:T(4,128)(2,1)} %copy-done.2, bf16[4,4096]{1,0:T(4,128)(2,1)S(1)} %collective-permute-done.10, bf16[4,4096]{1,0:T(4,128)(2,1)S(1)} %collective-permute-done.9, ...), dimensions={0} | concatenate | bytes 2097152 | tf_op jit(solution)/shard_map/jit(_roll_dynamic)/concatenate | solution.py:157
  295.5 1.5 fusion.28
  296.9 1.7 copy.57
  (224 shorter events, 58.7 us)
Async XLA Ops:
  1.4 3.2 %copy-start.10 = (s32[128]{0:T(128)}, s32[128]{0:T(128)S(1)}, u32[]{:S(2)}) copy-start(s32[128]{0:T(128)S(1)} %reshape_squeeze.7) | copy-start | bytes 1540
  4.7 11.2 %copy-start.15 = (s32[128]{0:T(128)}, s32[128]{0:T(128)S(1)}, u32[]{:S(2)}) copy-start(s32[128]{0:T(128)S(1)} %fusion.47) | copy-start | bytes 1540
  6.4 139.8 %all-to-all-start = ((bf16[16,16,4]{1,2,0:T(4,128)(2,1)}), bf16[16,16,4]{1,2,0:T(4,128)(2,1)}, u32[]{:S(2)}, u32[]{:S(2)}) async-start(bf16[16,16,4]{1,2,0:T(4,128)(2,1)} %copy.45), calls=%async_computation | async-start | bytes 32768 | tf_op jit(solution)/shard_map/all_to_all | solution.py:132
  51.8 2.4 copy-start.1
  54.1 1.3 copy-start.5
  54.1 1.3 copy-start.8
  63.1 1.8 copy-start.6
  63.1 1.8 copy-start.9
  64.9 1.3 copy-start.5
  64.9 1.3 copy-start.8
  73.9 1.0 copy-start.7
  73.9 1.8 copy-start.6
  73.9 1.8 copy-start.9
  75.7 1.3 copy-start.5
  75.7 1.3 copy-start.8
  84.7 1.0 copy-start.7
  84.7 1.8 copy-start.6
  84.7 1.8 copy-start.9
  86.5 1.3 copy-start.5
  86.5 1.3 copy-start.8
  95.4 1.0 copy-start.7
  95.4 1.8 copy-start.6
  95.5 1.8 copy-start.9
  97.3 1.3 copy-start.5
  97.3 1.3 copy-start.8
  106.2 1.0 copy-start.7
  106.2 1.8 copy-start.6
  106.2 1.8 copy-start.9
  108.0 1.3 copy-start.5
  108.0 1.3 copy-start.8
  117.0 1.0 copy-start.7
  117.0 1.8 copy-start.6
  117.0 1.8 copy-start.9
  118.8 1.3 copy-start.5
  118.8 1.3 copy-start.8
  127.8 1.8 copy-start.6
  127.8 1.8 copy-start.9
  129.6 1.3 copy-start.5
  129.6 1.3 copy-start.8
  138.6 1.0 copy-start.7
  138.6 1.8 copy-start.6
  138.6 1.8 copy-start.9
  146.2 47.1 %all-to-all-start.1 = ((bf16[16,16,4096]{2,1,0:T(8,128)(2,1)}), bf16[16,16,4096]{2,1,0:T(8,128)(2,1)}, u32[]{:S(2)}, u32[]{:S(2)}) async-start(bf16[16,16,4096]{2,1,0:T(8,128)(2,1)} %bitcast.7), calls=%async_computation.1 | async-start | bytes 4194304 | tf_op jit(solution)/shard_map/all_to_all | solution.py:118
  152.2 133.0 %copy-start.11 = (s32[128]{0:T(128)S(1)}, s32[128]{0:T(128)}, u32[]{:S(2)}) copy-start(s32[128]{0:T(128)} %copy-done.10) | copy-start | bytes 1540
  152.2 133.0 %copy-start.14 = (s32[128]{0:T(128)S(1)}, s32[128]{0:T(128)}, u32[]{:S(2)}) copy-start(s32[128]{0:T(128)} %copy-done.13) | copy-start | bytes 1540
  152.2 133.0 %copy-start.12 = (f32[1,8]{1,0:T(1,128)S(1)}, f32[1,8]{1,0:T(1,128)}, u32[]{:S(2)}) copy-start(f32[1,8]{1,0:T(1,128)} %param.13) | copy-start | bytes 100
  153.1 142.4 %copy-start = (f32[8,16,32,128]{3,2,1,0:T(8,128)S(1)}, f32[8,16,32,128]{3,2,1,0:T(8,128)}, u32[]{:S(2)}) copy-start(f32[8,16,32,128]{3,2,1,0:T(8,128)} %get-tuple-element.49) | copy-start | bytes 6291460
  195.3 11.4 %collective-permute-start = (bf16[4,4096]{1,0:T(4,128)(2,1)S(1)}, bf16[4,4096]{1,0:T(4,128)(2,1)S(1)}, u32[]{:S(2)}, u32[]{:S(2)}) collective-permute-start(bf16[4,4096]{1,0:T(4,128)(2,1)S(1)} %fusion.27), channel_id=1, source_target_pairs={{0,1},{1,2},{2,3},{3,4},{4,5},{5,6},{6,7},{7,8},{8,9},{9,10},{10,1... | collective-permute-start | bytes 98312 | tf_op jit(solution)/shard_map/ppermute | solution.py:154
  206.7 6.0 %collective-permute-start.1 = (bf16[4,4096]{1,0:T(4,128)(2,1)S(1)}, bf16[4,4096]{1,0:T(4,128)(2,1)S(1)}, u32[]{:S(2)}, u32[]{:S(2)}) collective-permute-start(bf16[4,4096]{1,0:T(4,128)(2,1)S(1)} %collective-permute-done), channel_id=1, source_target_pairs={{0,1},{1,2},{2,3},{3,4},{4,5},{5,6},{6,7},{7,8},{8,9},{9,10},{10,1... | collective-permute-start | bytes 98312 | tf_op jit(solution)/shard_map/ppermute | solution.py:154
  212.7 6.0 %collective-permute-start.2 = (bf16[4,4096]{1,0:T(4,128)(2,1)S(1)}, bf16[4,4096]{1,0:T(4,128)(2,1)S(1)}, u32[]{:S(2)}, u32[]{:S(2)}) collective-permute-start(bf16[4,4096]{1,0:T(4,128)(2,1)S(1)} %collective-permute-done.1), channel_id=1, source_target_pairs={{0,1},{1,2},{2,3},{3,4},{4,5},{5,6},{6,7},{7,8},{8,9},{9,10},{10,1... | collective-permute-start | bytes 98312 | tf_op jit(solution)/shard_map/ppermute | solution.py:154
  218.8 6.0 %collective-permute-start.3 = (bf16[4,4096]{1,0:T(4,128)(2,1)S(1)}, bf16[4,4096]{1,0:T(4,128)(2,1)S(1)}, u32[]{:S(2)}, u32[]{:S(2)}) collective-permute-start(bf16[4,4096]{1,0:T(4,128)(2,1)S(1)} %collective-permute-done.2), channel_id=1, source_target_pairs={{0,1},{1,2},{2,3},{3,4},{4,5},{5,6},{6,7},{7,8},{8,9},{9,10},{10,1... | collective-permute-start | bytes 98312 | tf_op jit(solution)/shard_map/ppermute | solution.py:154
  224.8 6.0 %collective-permute-start.4 = (bf16[4,4096]{1,0:T(4,128)(2,1)S(1)}, bf16[4,4096]{1,0:T(4,128)(2,1)S(1)}, u32[]{:S(2)}, u32[]{:S(2)}) collective-permute-start(bf16[4,4096]{1,0:T(4,128)(2,1)S(1)} %collective-permute-done.3), channel_id=1, source_target_pairs={{0,1},{1,2},{2,3},{3,4},{4,5},{5,6},{6,7},{7,8},{8,9},{9,10},{10,1... | collective-permute-start | bytes 98312 | tf_op jit(solution)/shard_map/ppermute | solution.py:154
  230.9 6.0 %collective-permute-start.5 = (bf16[4,4096]{1,0:T(4,128)(2,1)S(1)}, bf16[4,4096]{1,0:T(4,128)(2,1)S(1)}, u32[]{:S(2)}, u32[]{:S(2)}) collective-permute-start(bf16[4,4096]{1,0:T(4,128)(2,1)S(1)} %collective-permute-done.4), channel_id=1, source_target_pairs={{0,1},{1,2},{2,3},{3,4},{4,5},{5,6},{6,7},{7,8},{8,9},{9,10},{10,1... | collective-permute-start | bytes 98312 | tf_op jit(solution)/shard_map/ppermute | solution.py:154
  236.9 6.0 %collective-permute-start.6 = (bf16[4,4096]{1,0:T(4,128)(2,1)S(1)}, bf16[4,4096]{1,0:T(4,128)(2,1)S(1)}, u32[]{:S(2)}, u32[]{:S(2)}) collective-permute-start(bf16[4,4096]{1,0:T(4,128)(2,1)S(1)} %collective-permute-done.5), channel_id=1, source_target_pairs={{0,1},{1,2},{2,3},{3,4},{4,5},{5,6},{6,7},{7,8},{8,9},{9,10},{10,1... | collective-permute-start | bytes 98312 | tf_op jit(solution)/shard_map/ppermute | solution.py:154
  242.9 6.0 %collective-permute-start.7 = (bf16[4,4096]{1,0:T(4,128)(2,1)S(1)}, bf16[4,4096]{1,0:T(4,128)(2,1)S(1)}, u32[]{:S(2)}, u32[]{:S(2)}) collective-permute-start(bf16[4,4096]{1,0:T(4,128)(2,1)S(1)} %collective-permute-done.6), channel_id=1, source_target_pairs={{0,1},{1,2},{2,3},{3,4},{4,5},{5,6},{6,7},{7,8},{8,9},{9,10},{10,1... | collective-permute-start | bytes 98312 | tf_op jit(solution)/shard_map/ppermute | solution.py:154
  249.0 6.0 %collective-permute-start.8 = (bf16[4,4096]{1,0:T(4,128)(2,1)S(1)}, bf16[4,4096]{1,0:T(4,128)(2,1)S(1)}, u32[]{:S(2)}, u32[]{:S(2)}) collective-permute-start(bf16[4,4096]{1,0:T(4,128)(2,1)S(1)} %collective-permute-done.7), channel_id=1, source_target_pairs={{0,1},{1,2},{2,3},{3,4},{4,5},{5,6},{6,7},{7,8},{8,9},{9,10},{10,1... | collective-permute-start | bytes 98312 | tf_op jit(solution)/shard_map/ppermute | solution.py:154
  255.0 6.0 %collective-permute-start.9 = (bf16[4,4096]{1,0:T(4,128)(2,1)S(1)}, bf16[4,4096]{1,0:T(4,128)(2,1)S(1)}, u32[]{:S(2)}, u32[]{:S(2)}) collective-permute-start(bf16[4,4096]{1,0:T(4,128)(2,1)S(1)} %collective-permute-done.8), channel_id=1, source_target_pairs={{0,1},{1,2},{2,3},{3,4},{4,5},{5,6},{6,7},{7,8},{8,9},{9,10},{10,1... | collective-permute-start | bytes 98312 | tf_op jit(solution)/shard_map/ppermute | solution.py:154
  261.0 6.0 %collective-permute-start.10 = (bf16[4,4096]{1,0:T(4,128)(2,1)S(1)}, bf16[4,4096]{1,0:T(4,128)(2,1)S(1)}, u32[]{:S(2)}, u32[]{:S(2)}) collective-permute-start(bf16[4,4096]{1,0:T(4,128)(2,1)S(1)} %collective-permute-done.9), channel_id=1, source_target_pairs={{0,1},{1,2},{2,3},{3,4},{4,5},{5,6},{6,7},{7,8},{8,9},{9,10},{10,1... | collective-permute-start | bytes 98312 | tf_op jit(solution)/shard_map/ppermute | solution.py:154
  267.1 6.0 %collective-permute-start.11 = (bf16[4,4096]{1,0:T(4,128)(2,1)S(1)}, bf16[4,4096]{1,0:T(4,128)(2,1)S(1)}, u32[]{:S(2)}, u32[]{:S(2)}) collective-permute-start(bf16[4,4096]{1,0:T(4,128)(2,1)S(1)} %collective-permute-done.10), channel_id=1, source_target_pairs={{0,1},{1,2},{2,3},{3,4},{4,5},{5,6},{6,7},{7,8},{8,9},{9,10},{10,1... | collective-permute-start | bytes 98312 | tf_op jit(solution)/shard_map/ppermute | solution.py:154
  273.1 12.9 %copy-start.2 = (bf16[4,4096]{1,0:T(4,128)(2,1)}, bf16[4,4096]{1,0:T(4,128)(2,1)S(1)}, u32[]{:S(2)}) copy-start(bf16[4,4096]{1,0:T(4,128)(2,1)S(1)} %collective-permute-done.11) | copy-start | bytes 98308
  273.1 6.0 %collective-permute-start.12 = (bf16[4,4096]{1,0:T(4,128)(2,1)S(1)}, bf16[4,4096]{1,0:T(4,128)(2,1)S(1)}, u32[]{:S(2)}, u32[]{:S(2)}) collective-permute-start(bf16[4,4096]{1,0:T(4,128)(2,1)S(1)} %collective-permute-done.11), channel_id=1, source_target_pairs={{0,1},{1,2},{2,3},{3,4},{4,5},{5,6},{6,7},{7,8},{8,9},{9,10},{10,1... | collective-permute-start | bytes 98312 | tf_op jit(solution)/shard_map/ppermute | solution.py:154
  279.2 6.9 %copy-start.3 = (bf16[4,4096]{1,0:T(4,128)(2,1)}, bf16[4,4096]{1,0:T(4,128)(2,1)S(1)}, u32[]{:S(2)}) copy-start(bf16[4,4096]{1,0:T(4,128)(2,1)S(1)} %collective-permute-done.12) | copy-start | bytes 98308
  279.2 6.0 %collective-permute-start.13 = (bf16[4,4096]{1,0:T(4,128)(2,1)S(1)}, bf16[4,4096]{1,0:T(4,128)(2,1)S(1)}, u32[]{:S(2)}, u32[]{:S(2)}) collective-permute-start(bf16[4,4096]{1,0:T(4,128)(2,1)S(1)} %collective-permute-done.12), channel_id=1, source_target_pairs={{0,1},{1,2},{2,3},{3,4},{4,5},{5,6},{6,7},{7,8},{8,9},{9,10},{10,1... | collective-permute-start | bytes 98312 | tf_op jit(solution)/shard_map/ppermute | solution.py:154
  285.2 6.1 %collective-permute-start.14 = (bf16[4,4096]{1,0:T(4,128)(2,1)S(1)}, bf16[4,4096]{1,0:T(4,128)(2,1)}, u32[]{:S(2)}, u32[]{:S(2)}) collective-permute-start(bf16[4,4096]{1,0:T(4,128)(2,1)S(1)} %collective-permute-done.13), channel_id=1, source_target_pairs={{0,1},{1,2},{2,3},{3,4},{4,5},{5,6},{6,7},{7,8},{8,9},{9,10},{10,1... | collective-permute-start | bytes 98312 | tf_op jit(solution)/shard_map/ppermute | solution.py:154
  (4 other events, 3.3 us)
